TPU v7x, 32 devices: a whole 2x2x4 slice. The times are simulated.
32 devices in a mesh: dp: 8 (over z, x), mp: 4 (over y, core).
Axes of the slice: x: 2, y: 2, z: 4, core: 2. Of those that a mesh axis runs over, the one named last changes fastest.
Arguments:
- tokens: bfloat16 [2, 16384, 768], P(None, ('dp', 'mp')), may hold values from -6 to 6
- segment_ids: int32 [2, 16384], P(None, 'dp'), may hold values from 0 to 63, never falling along the last dimension, each value on 1 to 768 neighbouring positions
- norm1_gain: float32 [768], replicated, may hold values from 0.1 to 1.9
- norm1_bias: float32 [768], replicated, may hold values from -3 to 3
- w_qkv: bfloat16 [768, 3, 768], replicated, may hold values from -0.21875 to 0.21875
- conv_weight: float32 [3, 3, 768], P(None, None, 'mp'), may hold values from -3 to 3
- w_out: bfloat16 [768, 768], replicated, may hold values from -1.75 to 1.75
- norm2_gain: float32 [768], replicated, may hold values from 0.1 to 1.9
- norm2_bias: float32 [768], replicated, may hold values from -3 to 3
- w_in: bfloat16 [768, 3072], replicated, may hold values from -0.21875 to 0.21875
- w_down: bfloat16 [3072, 768], replicated, may hold values from -0.109375 to 0.109375
- cotangent: bfloat16 [2, 16384, 768], P(None, ('dp', 'mp')), may hold values from -6 to 6
Outputs:
- output: bfloat16 [2, 16384, 768], P(None, ('dp', 'mp'))
- input_grad: float32 [2, 16384, 768], P(None, ('dp', 'mp'))
- norm1_gain_grad: float32 [768], P('mp')
- norm1_bias_grad: float32 [768], P('mp')
- qkv_grad: float32 [768, 3, 768], P(None, None, 'mp')
- conv_grad: float32 [3, 3, 768], P(None, None, 'mp')
- out_grad: float32 [768, 768], P('mp')
- norm2_gain_grad: float32 [768], P('mp')
- norm2_bias_grad: float32 [768], P('mp')
- in_grad: float32 [768, 3072], replicated
- down_grad: float32 [3072, 768], replicated
Inputs may be any that keep to these rules, and one draw needn't show every extreme that they name: `segment_ids`: segment numbers never fall along a row of 16384 tokens. A document may run on past the end of a sequence of 1024 tokens, but attention and the convolution still stop there, whatever the numbers.
All inputs are finite; a program needn't handle non-finite values.
Results may differ from a plain program's by a relative error of at most 0.015.
The roundings to bfloat16 on the way count: a program that leaves them out, or rounds other values in their place, can miss the bound.
Values may be sent and summed in bfloat16 or wider, within the bound.
No kernel may reach another device: no remote copies, remote signals or barrier semaphores. Data moves between devices by JAX's collectives and lax.ppermute only.
A program may use at most 256 MiB of HBM per device.

v0:
```python
import math
import jax
import jax.numpy as jnp
from jax import lax
from jax.sharding import PartitionSpec as P

HEAD_DIM = 64
LEN = 1024
EPSILON = 1e-05
MASKED = -1e30


def normalize(values, norm_gain, norm_bias):
    centred = values - jnp.mean(values, axis=-1, keepdims=True)
    rstd_row = lax.rsqrt(jnp.mean(centred * centred, axis=-1, keepdims=True) + EPSILON)
    scaled = centred * rstd_row
    return (scaled * norm_gain + norm_bias, scaled, rstd_row)


def normalize_back(gradient, scaled, rstd_row, norm_gain):
    grad_scaled = gradient * norm_gain
    inner_term = (
        grad_scaled
        - jnp.mean(grad_scaled, axis=-1, keepdims=True)
        - scaled * jnp.mean(grad_scaled * scaled, axis=-1, keepdims=True)
    )
    return (rstd_row * inner_term, jnp.sum(gradient * scaled, axis=0), jnp.sum(gradient, axis=0))


def delayed(values, shift_by):
    widths = [(shift_by, 0)] + [(0, 0)] * (values.ndim - 1)
    return jnp.pad(values, widths)[: values.shape[0]]


def advanced(values, shift_by):
    widths = [(0, shift_by)] + [(0, 0)] * (values.ndim - 1)
    return jnp.pad(values, widths)[shift_by:]


def score_block(queries_all, keys_all, seg_seqs, block_id, block_rows, scaling):
    per_seq = LEN // block_rows
    seq_id = block_id // per_seq
    first_row = block_id % per_seq * block_rows
    query_seq = lax.dynamic_index_in_dim(queries_all, seq_id, 0, keepdims=False)
    queries = lax.dynamic_slice_in_dim(query_seq, first_row, block_rows, 0)
    key_seq = lax.dynamic_index_in_dim(keys_all, seq_id, 0, keepdims=False)
    seg_seq = lax.dynamic_index_in_dim(seg_seqs, seq_id, 0, keepdims=False)
    seg_query = lax.dynamic_slice_in_dim(seg_seq, first_row, block_rows, 0)
    rows_at = first_row + lax.iota(jnp.int32, block_rows)
    cols_at = lax.iota(jnp.int32, LEN)
    allowed = (cols_at[None, :] <= rows_at[:, None]) & (seg_seq[None, :] == seg_query[:, None])
    scores = (
        jnp.einsum("qhd,khd->hqk", queries, key_seq, preferred_element_type=jnp.float32) * scaling
    )
    return (jnp.where(allowed[None], scores, MASKED), queries, key_seq, seq_id, first_row)


def attend_forward(queries_all, keys_all, values_all, seg_seqs, block_rows, scaling):
    block_count = queries_all.shape[0] * (LEN // block_rows)

    def forward_block(block_id):
        scores, queries, key_seq, seq_id, first_row = score_block(
            queries_all, keys_all, seg_seqs, block_id, block_rows, scaling
        )
        value_seq = lax.dynamic_index_in_dim(values_all, seq_id, 0, keepdims=False)
        row_top = jnp.max(scores, axis=-1, keepdims=True)
        weights = jnp.exp(scores - row_top)
        row_total = jnp.sum(weights, axis=-1, keepdims=True)
        probabilities = (weights / row_total).astype(jnp.bfloat16)
        attended = jnp.einsum(
            "hqk,khd->qhd", probabilities, value_seq, preferred_element_type=jnp.float32
        )
        return (
            attended.astype(jnp.bfloat16).reshape(block_rows, -1),
            (row_top + jnp.log(row_total))[..., 0],
        )

    return lax.map(forward_block, jnp.arange(block_count, dtype=jnp.int32))


def attend_backward(
    queries_all, keys_all, values_all, seg_seqs, row_lse, grad_heads, block_rows, scaling
):
    seq_count = queries_all.shape[0]
    per_seq = LEN // block_rows
    grad_seqs = grad_heads.reshape(queries_all.shape)

    def backward_block(block_id):
        scores, queries, key_seq, seq_id, first_row = score_block(
            queries_all, keys_all, seg_seqs, block_id, block_rows, scaling
        )
        value_seq = lax.dynamic_index_in_dim(values_all, seq_id, 0, keepdims=False)
        grad_seq = lax.dynamic_index_in_dim(grad_seqs, seq_id, 0, keepdims=False)
        grad_rows = lax.dynamic_slice_in_dim(grad_seq, first_row, block_rows, 0)
        lse_block = lax.dynamic_index_in_dim(row_lse, block_id, 0, keepdims=False)
        probabilities = jnp.exp(scores - lse_block[..., None])
        grad_probs = jnp.einsum(
            "qhd,khd->hqk", grad_rows, value_seq, preferred_element_type=jnp.float32
        )
        row_dot = jnp.sum(probabilities * grad_probs, axis=-1, keepdims=True)
        grad_scores = (probabilities * (grad_probs - row_dot)).astype(jnp.bfloat16)
        grad_queries = (
            jnp.einsum("hqk,khd->qhd", grad_scores, key_seq, preferred_element_type=jnp.float32)
            * scaling
        )
        grad_keys = (
            jnp.einsum("hqk,qhd->khd", grad_scores, queries, preferred_element_type=jnp.float32)
            * scaling
        )
        grad_values = jnp.einsum(
            "hqk,qhd->khd",
            probabilities.astype(jnp.bfloat16),
            grad_rows,
            preferred_element_type=jnp.float32,
        )
        return (grad_queries, grad_keys, grad_values)

    grad_queries, grad_keys, grad_values = lax.map(
        backward_block, jnp.arange(seq_count * per_seq, dtype=jnp.int32)
    )
    key_shape = (seq_count, per_seq) + grad_keys.shape[1:]
    grad_keys = jnp.sum(grad_keys.reshape(key_shape), axis=1)
    grad_values = jnp.sum(grad_values.reshape(key_shape), axis=1)
    return (grad_queries, grad_keys, grad_values)


def local(
    tokens,
    segment_ids,
    norm1_gain,
    norm1_bias,
    w_qkv,
    conv_weight,
    w_out,
    norm2_gain,
    norm2_bias,
    w_in,
    w_down,
    cotangent,
):
    micro_count = tokens.shape[0]
    group_rows = segment_ids.shape[1]
    local_width = conv_weight.shape[2]
    local_heads = local_width // HEAD_DIM
    seq_count = group_rows // LEN
    block_rows = min(512, LEN)
    scaling = 1.0 / math.sqrt(HEAD_DIM)
    places = lax.iota(jnp.int32, group_rows) % LEN
    kept = []
    outputs = []
    for micro_step in range(micro_count):
        token_rows = tokens[micro_step].astype(jnp.float32)
        normed_one, scaled_one, rstd_one = normalize(token_rows, norm1_gain, norm1_bias)
        normed_one = normed_one.astype(jnp.bfloat16)
        projected = jnp.einsum(
            "rd,dce->rce", normed_one, w_qkv, preferred_element_type=jnp.float32
        ).astype(jnp.bfloat16)
        by_heads = lax.all_to_all(projected, "mp", split_axis=2, concat_axis=0, tiled=True)
        seg_row = segment_ids[micro_step]
        same_one = ((places >= 1) & (delayed(seg_row, 1) == seg_row)).astype(jnp.float32)[
            :, None, None
        ]
        same_two = ((places >= 2) & (delayed(seg_row, 2) == seg_row)).astype(jnp.float32)[
            :, None, None
        ]
        heads_wide = by_heads.astype(jnp.float32)
        mixed = (
            heads_wide * conv_weight[:, 0]
            + delayed(heads_wide, 1) * same_one * conv_weight[:, 1]
            + delayed(heads_wide, 2) * same_two * conv_weight[:, 2]
        ).astype(jnp.bfloat16)
        shaped = mixed.reshape(seq_count, LEN, 3, local_heads, HEAD_DIM)
        queries_all = shaped[:, :, 0]
        keys_all = shaped[:, :, 1]
        values_all = shaped[:, :, 2]
        seg_seqs = seg_row.reshape(seq_count, LEN)
        attended, row_lse = attend_forward(
            queries_all, keys_all, values_all, seg_seqs, block_rows, scaling
        )
        attended = attended.reshape(group_rows, local_width)
        by_tokens = lax.all_to_all(attended, "mp", split_axis=0, concat_axis=1, tiled=True)
        resid = token_rows + jnp.dot(by_tokens, w_out, preferred_element_type=jnp.float32)
        normed_two, scaled_two, rstd_two = normalize(resid, norm2_gain, norm2_bias)
        normed_two = normed_two.astype(jnp.bfloat16)
        hidden_pre = jnp.dot(normed_two, w_in, preferred_element_type=jnp.float32)
        hidden = (jnp.maximum(hidden_pre, 0.0) ** 2).astype(jnp.bfloat16)
        outputs.append(
            (resid + jnp.dot(hidden, w_down, preferred_element_type=jnp.float32)).astype(
                jnp.bfloat16
            )
        )
        kept.append(
            (
                normed_one,
                scaled_one,
                rstd_one,
                heads_wide,
                same_one,
                same_two,
                queries_all,
                keys_all,
                values_all,
                seg_seqs,
                row_lse,
                by_tokens,
                normed_two,
                scaled_two,
                rstd_two,
                hidden_pre,
                hidden,
            )
        )
    grad_qkv = jnp.zeros(w_qkv.shape, jnp.float32)
    grad_conv = jnp.zeros(conv_weight.shape, jnp.float32)
    grad_wout = jnp.zeros(w_out.shape, jnp.float32)
    grad_in = jnp.zeros(w_in.shape, jnp.float32)
    grad_down = jnp.zeros(w_down.shape, jnp.float32)
    gain_one_grad = jnp.zeros(norm1_gain.shape, jnp.float32)
    bias_one_grad = jnp.zeros(norm1_bias.shape, jnp.float32)
    gain_two_grad = jnp.zeros(norm2_gain.shape, jnp.float32)
    bias_two_grad = jnp.zeros(norm2_bias.shape, jnp.float32)
    input_grads = [None] * micro_count
    for micro_step in reversed(range(micro_count)):
        (
            normed_one,
            scaled_one,
            rstd_one,
            heads_wide,
            same_one,
            same_two,
            queries_all,
            keys_all,
            values_all,
            seg_seqs,
            row_lse,
            by_tokens,
            normed_two,
            scaled_two,
            rstd_two,
            hidden_pre,
            hidden,
        ) = kept[micro_step]
        grad_output = cotangent[micro_step]
        grad_down = grad_down + jnp.einsum(
            "rf,rd->fd", hidden, grad_output, preferred_element_type=jnp.float32
        )
        grad_hidden = jnp.einsum(
            "rd,fd->rf", grad_output, w_down, preferred_element_type=jnp.float32
        )
        grad_pre = (grad_hidden * 2.0 * jnp.maximum(hidden_pre, 0.0)).astype(jnp.bfloat16)
        grad_in = grad_in + jnp.einsum(
            "rd,rf->df", normed_two, grad_pre, preferred_element_type=jnp.float32
        )
        grad_normed_two = jnp.einsum(
            "rf,df->rd", grad_pre, w_in, preferred_element_type=jnp.float32
        )
        back_two, gain_two_part, bias_two_part = normalize_back(
            grad_normed_two, scaled_two, rstd_two, norm2_gain
        )
        gain_two_grad = gain_two_grad + gain_two_part
        bias_two_grad = bias_two_grad + bias_two_part
        grad_resid = grad_output.astype(jnp.float32) + back_two
        grad_branch = grad_resid.astype(jnp.bfloat16)
        grad_wout = grad_wout + jnp.einsum(
            "re,rd->ed", by_tokens, grad_branch, preferred_element_type=jnp.float32
        )
        grad_attended = jnp.einsum(
            "rd,ed->re", grad_branch, w_out, preferred_element_type=jnp.float32
        ).astype(jnp.bfloat16)
        grad_heads = lax.all_to_all(grad_attended, "mp", split_axis=1, concat_axis=0, tiled=True)
        grad_queries, grad_keys, grad_values = attend_backward(
            queries_all, keys_all, values_all, seg_seqs, row_lse, grad_heads, block_rows, scaling
        )
        grad_mixed = jnp.stack(
            [
                grad_queries.reshape(group_rows, local_width),
                grad_keys.reshape(group_rows, local_width),
                grad_values.reshape(group_rows, local_width),
            ],
            axis=1,
        )
        weighted_one = grad_mixed * same_one
        weighted_two = grad_mixed * same_two
        grad_conv = grad_conv + jnp.stack(
            [
                jnp.sum(grad_mixed * heads_wide, axis=0),
                jnp.sum(weighted_one * delayed(heads_wide, 1), axis=0),
                jnp.sum(weighted_two * delayed(heads_wide, 2), axis=0),
            ],
            axis=1,
        )
        grad_proj = (
            grad_mixed * conv_weight[:, 0]
            + advanced(weighted_one, 1) * conv_weight[:, 1]
            + advanced(weighted_two, 2) * conv_weight[:, 2]
        ).astype(jnp.bfloat16)
        grad_tokens = lax.all_to_all(grad_proj, "mp", split_axis=0, concat_axis=2, tiled=True)
        grad_qkv = grad_qkv + jnp.einsum(
            "rd,rce->dce", normed_one, grad_tokens, preferred_element_type=jnp.float32
        )
        grad_normed_one = jnp.einsum(
            "rce,dce->rd", grad_tokens, w_qkv, preferred_element_type=jnp.float32
        )
        back_one, gain_one_part, bias_one_part = normalize_back(
            grad_normed_one, scaled_one, rstd_one, norm1_gain
        )
        gain_one_grad = gain_one_grad + gain_one_part
        bias_one_grad = bias_one_grad + bias_one_part
        input_grads[micro_step] = grad_resid + back_one
    head_parts = (
        lax.psum_scatter(
            grad_qkv.astype(jnp.bfloat16), "mp", scatter_dimension=2, tiled=True
        ).astype(jnp.float32),
        lax.psum_scatter(
            grad_wout.astype(jnp.bfloat16), "mp", scatter_dimension=0, tiled=True
        ).astype(jnp.float32),
        lax.psum_scatter(
            gain_one_grad.astype(jnp.bfloat16), "mp", scatter_dimension=0, tiled=True
        ).astype(jnp.float32),
        lax.psum_scatter(
            bias_one_grad.astype(jnp.bfloat16), "mp", scatter_dimension=0, tiled=True
        ).astype(jnp.float32),
        lax.psum_scatter(
            gain_two_grad.astype(jnp.bfloat16), "mp", scatter_dimension=0, tiled=True
        ).astype(jnp.float32),
        lax.psum_scatter(
            bias_two_grad.astype(jnp.bfloat16), "mp", scatter_dimension=0, tiled=True
        ).astype(jnp.float32),
    )
    head_total = lax.psum(
        (
            head_parts[0],
            head_parts[1],
            grad_conv,
            head_parts[2],
            head_parts[3],
            head_parts[4],
            head_parts[5],
        ),
        "dp",
    )
    dense_parts = (
        lax.psum_scatter(grad_in, ("dp", "mp"), scatter_dimension=1, tiled=True),
        lax.psum_scatter(grad_down, ("dp", "mp"), scatter_dimension=0, tiled=True),
    )
    dense_total = (
        lax.all_gather(
            dense_parts[0].astype(jnp.bfloat16), ("dp", "mp"), axis=1, tiled=True
        ).astype(jnp.float32),
        lax.all_gather(
            dense_parts[1].astype(jnp.bfloat16), ("dp", "mp"), axis=0, tiled=True
        ).astype(jnp.float32),
    )
    return (
        jnp.stack(outputs, axis=0),
        jnp.stack(input_grads, axis=0),
        head_total[3],
        head_total[4],
        head_total[0],
        head_total[2],
        head_total[1],
        head_total[5],
        head_total[6],
        dense_total[0],
        dense_total[1],
    )


def solution(mesh):
    placed = (
        P(None, ("dp", "mp"), None),
        P(None, "dp"),
        P(),
        P(),
        P(),
        P(None, None, "mp"),
        P(),
        P(),
        P(),
        P(),
        P(),
        P(None, ("dp", "mp"), None),
    )
    return jax.shard_map(
        local,
        mesh=mesh,
        in_specs=placed,
        out_specs=(
            P(None, ("dp", "mp"), None),
            P(None, ("dp", "mp"), None),
            P("mp"),
            P("mp"),
            P(None, None, "mp"),
            P(None, None, "mp"),
            P("mp", None),
            P("mp"),
            P("mp"),
            P(),
            P(),
        ),
        check_vma=False,
    )
```

profile of v0, /device:TPU:0, one launch (start us, length us, event | category | flops | bytes accessed | tf_op | source)
XLA Modules:
  0.0 973.8 jit_solution(13896892952462681706)
XLA Ops:
  15.4 6.0 copy.62
  21.4 4.6 all-to-all-start
  26.6 4.7 convolution_convert_fusion
  31.3 6.0 copy.68
  37.3 26.4 %all-to-all-done = bf16[512,3,768]{0,1,2:T(4,128)(2,1)} async-done(((bf16[512,3,768]{0,1,2:T(4,128)(2,1)}), bf16[512,3,768]{0,1,2:T(4,128)(2,1)}, u32[]{:S(2)}, u32[]{:S(2)}) %all-to-all-start) | async-done | bytes 2359328 | tf_op jit(solution)/shard_map/all_to_all | solution.py:158
  63.7 4.9 all-to-all-start.2
  82.7 22.8 %all-to-all-done.2 = bf16[512,3,768]{0,1,2:T(4,128)(2,1)} async-done(((bf16[512,3,768]{0,1,2:T(4,128)(2,1)}), bf16[512,3,768]{0,1,2:T(4,128)(2,1)}, u32[]{:S(2)}, u32[]{:S(2)}) %all-to-all-start.2) | async-done | bytes 2359328 | tf_op jit(solution)/shard_map/all_to_all | solution.py:158
  112.2 7.5 add_convert_fusion.2
  119.7 6.6 reshape.593
  134.7 49.8 %while.64 = (s32[]{:T(128)}, bf16[4,512,192]{1,2,0:T(8,128)(2,1)}, f32[4,3,512]{2,1,0:T(4,128)}, s32[4]{0:T(128)}, bf16[2,1024,3,64]{1,3,2,0:T(8,128)(2,1)}, /*i...) while((s32[]{:T(128)}, bf16[4,512,192]{1,2,0:T(8,128)(2,1)}, ...), condition=%wide.region_5.6_spmd, body=%wide.region_2.5_spmd.sunk | while | flops 423197728 | bytes 25768452 | solution.py:78
  188.7 6.6 reshape.594
  203.8 49.4 %while.65 = (s32[]{:T(128)}, bf16[4,512,192]{1,2,0:T(8,128)(2,1)}, f32[4,3,512]{2,1,0:T(4,128)}, s32[4]{0:T(128)}, bf16[2,1024,3,64]{1,3,2,0:T(8,128)(2,1)}, /*i...) while((s32[]{:T(128)}, bf16[4,512,192]{1,2,0:T(8,128)(2,1)}, ...), condition=%wide.region_13.14_spmd, body=%wide.region_10.13_spmd.sunk | while | flops 423197728 | bytes 25768452 | solution.py:78
  253.3 4.2 all-to-all-start.3
  262.3 6.8 all-to-all-done.3
  272.3 4.9 fusion.234
  280.1 8.6 multiply_convert_fusion.2
  288.7 5.2 multiply_convert_fusion.3
  294.0 5.8 fusion.233
  299.8 5.6 convolution_add_fusion.1
  305.5 6.1 fusion.239
  311.7 6.7 multiply_reduce_fusion.6
  325.8 4.2 all-to-all-start.4
  336.0 5.3 fusion.168
  341.3 9.5 convolution_add_fusion
  350.8 4.6 all-to-all-start.6
  369.1 79.1 %while.66 = (s32[]{:T(128)}, f32[4,512,3,64]{1,3,2,0:T(8,128)}, f32[4,1024,3,64]{1,3,2,0:T(8,128)}, f32[4,1024,3,64]{1,3,2,0:T(8,128)}, s32[4]{0:T(128)S(1)}, /*...) while((s32[]{:T(128)}, f32[4,512,3,64]{1,3,2,0:T(8,128)}, ...), condition=%wide.region_20.21_spmd, body=%wide.region_18.20_spmd.sunk | while | flops 1032092672 | bytes 62722712 | solution.py:118
  461.8 79.5 %while.67 = (s32[]{:T(128)}, f32[4,512,3,64]{1,3,2,0:T(8,128)}, f32[4,1024,3,64]{1,3,2,0:T(8,128)}, f32[4,1024,3,64]{1,3,2,0:T(8,128)}, s32[4]{0:T(128)S(1)}, /*...) while((s32[]{:T(128)}, f32[4,512,3,64]{1,3,2,0:T(8,128)}, ...), condition=%wide.region_29.30_spmd, body=%wide.region_27.29_spmd.sunk | while | flops 1032092672 | bytes 62722712 | solution.py:118
  592.5 5.9 multiply_reduce_fusion.5
  598.5 6.6 multiply_reduce_fusion.3
  605.1 10.6 %fusion.111 = (bf16[2048,3,192]{0,2,1:T(8,128)(2,1)}, bf16[2048,3,192]{0,2,1:T(8,128)(2,1)}) fusion(f32[2048,3,192]{0,2,1:T(8,128)} %get-tuple-element.888, f32[2048,3,192]{0,2,1:T(8,128)} %get-tuple-element.887, f32[2048,3,192]{0,2,1:T(8,128)S(1)} %constant_dynamic-update-slice_fusion.2, f32[3,192]{1,0:T(4,128)S(1)} %copy-done.63, ...), kind=kLoop, calls=%fused_computation.154 | loop fusion | flops 14155776 | bytes 33037056 | tf_op jit(solution)/shard_map/convert_element_type | solution.py:296
  615.7 7.0 copy.83
  622.7 4.9 all-to-all-start.5
  627.5 6.9 copy.96
  634.5 41.3 %all-to-all-done.5 = bf16[2048,3,192]{2,1,0:T(4,128)(2,1)} async-done(((bf16[2048,3,192]{2,1,0:T(4,128)(2,1)}), bf16[2048,3,192]{2,1,0:T(4,128)(2,1)}, u32[]{:S(2)}, u32[]{:S(2)}) %all-to-all-start.5) | async-done | bytes 2359328 | tf_op jit(solution)/shard_map/all_to_all | solution.py:297
  675.7 4.9 all-to-all-start.7
  686.3 6.9 copy.85
  693.3 41.9 %all-to-all-done.7 = bf16[2048,3,192]{2,1,0:T(4,128)(2,1)} async-done(((bf16[2048,3,192]{2,1,0:T(4,128)(2,1)}), bf16[2048,3,192]{2,1,0:T(4,128)(2,1)}, u32[]{:S(2)}, u32[]{:S(2)}) %all-to-all-start.7) | async-done | bytes 2359328 | tf_op jit(solution)/shard_map/all_to_all | solution.py:297
  735.2 7.0 copy.98
  742.3 4.5 fusion.170
  746.8 4.4 add_convert_fusion
  755.9 8.9 fusion.167
  764.8 6.8 fusion.166
  800.5 5.1 fusion.154
  806.9 6.5 all-reduce.17
  827.2 118.0 %all-reduce.19 = (f32[192]{0:T(256)}, f32[192]{0:T(256)}, f32[768,3,192]{0,2,1:T(8,128)}, f32[3,3,192]{2,0,1:T(4,128)}, f32[192,768]{1,0:T(8,128)}, /*index=5*/f32[192]{0:T(256)}, f32[192]{0:T(256)}) all-reduce(f32[192]{0:T(256)S(1)} %copy-done.91, f32[192]{0:T(256)} %dynamic-slice_convert_fusion.2, ...), channel_id=1, replica_groups=mesh['dp'=8,'mp'=4] {'dp'}, use_global_device_ids=true, to_apply=%region_37.38 | all-reduce | flops 592320 | bytes 3558912 | tf_op jit(solution)/shard_map/psum | solution.py:330
  946.5 7.5 copy.109
  954.0 5.7 all-gather.5.cloned.1.call-done
  959.7 6.8 convert_element_type.321
  (585 shorter events, 411.4 us)
Async XLA Ops:
  9.0 17.0 %copy-start.70 = (f32[512]{0:T(512)}, f32[512]{0:T(512)S(1)}, u32[]{:S(2)}) copy-start(f32[512]{0:T(512)S(1)} %get-tuple-element.932) | copy-start | bytes 6148
  21.4 42.3 %all-to-all-start = ((bf16[512,3,768]{0,1,2:T(4,128)(2,1)}), bf16[512,3,768]{0,1,2:T(4,128)(2,1)}, u32[]{:S(2)}, u32[]{:S(2)}) async-start(bf16[512,3,768]{0,1,2:T(4,128)(2,1)} %copy.62), calls=%async_computation | async-start | bytes 6291456 | tf_op jit(solution)/shard_map/all_to_all | solution.py:158
  37.3 31.3 %copy-start.87 = (f32[3,3,192]{2,1,0:T(4,128)S(1)}, f32[3,3,192]{2,1,0:T(4,128)}, u32[]{:S(2)}) copy-start(f32[3,3,192]{2,1,0:T(4,128)} %param.25) | copy-start | bytes 20740
  63.7 41.8 %all-to-all-start.2 = ((bf16[512,3,768]{0,1,2:T(4,128)(2,1)}), bf16[512,3,768]{0,1,2:T(4,128)(2,1)}, u32[]{:S(2)}, u32[]{:S(2)}) async-start(bf16[512,3,768]{0,1,2:T(4,128)(2,1)} %copy.68), calls=%async_computation.2 | async-start | bytes 6291456 | tf_op jit(solution)/shard_map/all_to_all | solution.py:158
  110.7 9.0 copy-start.3
  184.5 68.8 %all-to-all-start.1 = ((bf16[4,512,192]{1,2,0:T(8,128)(2,1)}), bf16[4,512,192]{1,2,0:T(8,128)(2,1)}, u32[]{:S(2)}, u32[]{:S(2)}) async-start(bf16[4,512,192]{1,2,0:T(8,128)(2,1)} %get-tuple-element.653), calls=%async_computation.1 | async-start | bytes 1572864 | tf_op jit(solution)/shard_map/all_to_all | solution.py:181
  253.2 7.1 copy-start.45
  253.3 15.9 %all-to-all-start.3 = ((bf16[4,512,192]{1,2,0:T(8,128)(2,1)}), bf16[4,512,192]{1,2,0:T(8,128)(2,1)}, u32[]{:S(2)}, u32[]{:S(2)}) async-start(bf16[4,512,192]{1,2,0:T(8,128)(2,1)} %get-tuple-element.654), calls=%async_computation.3 | async-start | bytes 1572864 | tf_op jit(solution)/shard_map/all_to_all | solution.py:181
  257.5 493.8 %reduce-scatter.9.cloned.1.call-start = ((), (), s32[]{:S(2)}) async-start(), calls=%async_computation.14 | async-start | bytes 9732096 | tf_op jit(solution)/shard_map/reduce_scatter | solution.py:343
  269.2 8.1 slice-start.6
  271.9 22.0 %copy-start.29 = (f32[512,768]{1,0:T(8,128)}, f32[512,768]{1,0:T(8,128)S(1)}, u32[]{:S(2)}) copy-start(f32[512,768]{1,0:T(8,128)S(1)} %get-tuple-element.927) | copy-start | bytes 4718596
  271.9 22.0 %copy-start.68 = (f32[512]{0:T(512)}, f32[512]{0:T(512)S(1)}, u32[]{:S(2)}) copy-start(f32[512]{0:T(512)S(1)} %broadcast_multiply_fusion.12) | copy-start | bytes 6148
  272.3 21.7 %copy-start.85 = (f32[512]{0:T(512)}, f32[512]{0:T(512)S(1)}, u32[]{:S(2)}) copy-start(f32[512]{0:T(512)S(1)} %add_rsqrt_fusion) | copy-start | bytes 6148
  280.1 8.6 copy-start.8
  294.0 5.8 copy-start.40
  305.5 6.2 copy-start.18
  305.5 6.2 copy-start.30
  305.5 6.1 copy-start.41
  305.5 6.1 copy-start.59
  305.5 6.1 copy-start.67
  305.5 6.1 copy-start.69
  305.5 6.1 copy-start.86
  311.7 6.7 copy-start.27
  325.8 25.0 %all-to-all-start.4 = ((bf16[512,4,192]{0,2,1:T(8,128)(2,1)}), bf16[512,4,192]{0,2,1:T(8,128)(2,1)}, u32[]{:S(2)}, u32[]{:S(2)}) async-start(bf16[512,4,192]{0,2,1:T(8,128)(2,1)} %bitcast.519), calls=%async_computation.4 | async-start | bytes 1572864 | tf_op jit(solution)/shard_map/all_to_all | solution.py:270
  330.0 423.0 %reduce-scatter.11.cloned.1.call-start = ((), (), s32[]{:S(2)}) async-start(), calls=%async_computation.16 | async-start | bytes 9732096 | tf_op jit(solution)/shard_map/reduce_scatter | solution.py:344
  336.0 5.3 copy-start.28
  350.8 97.4 %all-to-all-start.6 = ((bf16[512,4,192]{0,2,1:T(8,128)(2,1)}), bf16[512,4,192]{0,2,1:T(8,128)(2,1)}, u32[]{:S(2)}, u32[]{:S(2)}) async-start(bf16[512,4,192]{0,2,1:T(8,128)(2,1)} %bitcast.518), calls=%async_computation.6 | async-start | bytes 1572864 | tf_op jit(solution)/shard_map/all_to_all | solution.py:270
  541.3 5.0 copy-start.20
  586.5 5.8 slice-start.4
  591.7 6.7 slice-start.2
  592.5 6.0 slice-start.3
  592.5 6.0 copy-start.49
  592.5 6.0 copy-start.51
  598.4 6.6 copy-start.61
  598.4 6.6 copy-start.63
  598.5 6.6 copy-start.65
  622.7 53.1 %all-to-all-start.5 = ((bf16[2048,3,192]{2,1,0:T(4,128)(2,1)}), bf16[2048,3,192]{2,1,0:T(4,128)(2,1)}, u32[]{:S(2)}, u32[]{:S(2)}) async-start(bf16[2048,3,192]{2,1,0:T(4,128)(2,1)} %copy.83), calls=%async_computation.5 | async-start | bytes 8388608 | tf_op jit(solution)/shard_map/all_to_all | solution.py:297
  675.7 59.4 %all-to-all-start.7 = ((bf16[2048,3,192]{2,1,0:T(4,128)(2,1)}), bf16[2048,3,192]{2,1,0:T(4,128)(2,1)}, u32[]{:S(2)}, u32[]{:S(2)}) async-start(bf16[2048,3,192]{2,1,0:T(4,128)(2,1)} %copy.96), calls=%async_computation.7 | async-start | bytes 8388608 | tf_op jit(solution)/shard_map/all_to_all | solution.py:297
  680.6 115.9 %reduce-scatter.7.cloned.1.call-start = ((), (), s32[]{:S(2)}) async-start(), calls=%async_computation.13 | async-start | bytes 1474560 | tf_op jit(solution)/shard_map/reduce_scatter | solution.py:314
  686.3 140.9 %reduce-scatter.5.cloned.1.call-start = ((), (), s32[]{:S(2)}) async-start(), calls=%async_computation.12 | async-start | bytes 4423680 | tf_op jit(solution)/shard_map/reduce_scatter | solution.py:311
  735.2 7.0 copy-start.71
  735.2 7.1 copy-start.83
  735.2 7.1 copy-start.89
  735.2 7.1 copy-start.98
  751.2 195.3 %all-gather.3.cloned.1.call-start = ((), (), s32[]{:S(2)}) async-start(), calls=%async_computation.15 | async-start | bytes 4866048 | tf_op jit(solution)/shard_map/all_gather | solution.py:347
  752.9 206.8 %all-gather.5.cloned.1.call-start = ((), (), s32[]{:S(2)}) async-start(), calls=%async_computation.17 | async-start | bytes 4866048 | tf_op jit(solution)/shard_map/all_gather | solution.py:350
  755.9 8.9 copy-start.19
  800.5 5.1 copy-start.44
  (98 other events, 241.4 us)
Sparse Core Ops, SparseCore 0:
  305.6 141.4 reduce-scatter.8
  453.6 135.1 reduce-scatter.10
  686.4 34.4 reduce-scatter.6
  751.3 41.3 reduce-scatter.4
  795.5 82.9 all-gather.2
  881.2 78.4 all-gather.4
where the time goes:
time: 984 us; the launch traced here: 974 us
  matrix products  254 us (26%)
  local copies, waits for them, and re-layouts  225 us (23%)
  waiting for transfers between devices  145 us (15%)
  blocking collectives  125 us (13%)
  other arithmetic  118 us (12%)
  loops' own time  53.9 us (5%)
  starting transfers between devices  36.9 us (4%)
  between operations  16.6 us (2%)
    psum x1, blocking collectives, local(): lax.psum((head_parts[0], head_parts[1], grad_conv, head_parts[2], head_pa...  118 us
    all_to_all x2, waiting for transfers between devices, local(): lax.all_to_all(grad_proj, 'mp', split_axis=0, concat_axis=2, tiled=True)  83.2 us
    all_to_all x2, waiting for transfers between devices, local(): lax.all_to_all(projected, 'mp', split_axis=2, concat_axis=0, tiled=True)  49.3 us
    dot_general x16, matrix products, score_block(): jnp.einsum('qhd,khd->hqk', queries, key_seq, preferred_element_type=jnp.f...  39.8 us
    another operation x16, local copies, waits for them, and re-layouts, local(): jnp.stack([grad_queries.reshape(group_rows, local_width), grad_keys.resha...  39 us
    another operation x2, loops' own time, attend_backward(): lax.map(backward_block, jnp.arange(seq_count * per_seq, dtype=jnp.int32))  32.2 us
    unnamed x209, local copies, waits for them, and re-layouts  27.9 us
    dot_general x8, matrix products, backward_block(): jnp.einsum('hqk,qhd->khd', probabilities.astype(jnp.bfloat16), grad_rows,...  22.4 us
  transfers between devices with their start and end apart: 14, of which 6 were waited for; matrix products, arithmetic and copies ran while one was open for 48% of the time, Pallas kernels for 0%

commit v1 on v0

--- a/solution.py
+++ b/solution.py
@@ -294,7 +294,15 @@
             + advanced(weighted_one, 1) * conv_weight[:, 1]
             + advanced(weighted_two, 2) * conv_weight[:, 2]
         ).astype(jnp.bfloat16)
-        grad_tokens = lax.all_to_all(grad_proj, "mp", split_axis=0, concat_axis=2, tiled=True)
+
+        def link_unit(z):
+            front = lax.axis_size("mp")
+            vec_out = jnp.split(z, front, 0)
+            view_out = jnp.stack(vec_out, 0)
+            a_now = lax.all_to_all(view_out, axis_name="mp", split_axis=0, concat_axis=0)
+            return jnp.concatenate(a_now, 2)
+
+        grad_tokens = link_unit(grad_proj)
         grad_qkv = grad_qkv + jnp.einsum(
             "rd,rce->dce", normed_one, grad_tokens, preferred_element_type=jnp.float32
         )

time: 984 us -> 927 us (0.942)
  waiting for transfers between devices: 145 us -> 109 us
  local copies, waits for them, and re-layouts: 225 us -> 204 us
    all_to_all x2, waiting for transfers between devices: 83.2 us -> 47.2 us  [link_unit(): lax.all_to_all(view_out, axis_name='mp', split_axis=0, concat_axis=0)]
    all_to_all x2 -> x0, local copies, waits for them, and re-layouts: 14 us -> none  [local(): lax.all_to_all(grad_proj, 'mp', split_axis=0, concat_axis=2, tiled=True)]
    convert_element_type x2 -> x0, local copies, waits for them, and re-layouts: 13.9 us -> none  [local(): grad_proj = (grad_mixed * conv_weight[:, 0] + advanced(weighted_one, 1) *...]
    unnamed x209 -> x211, local copies, waits for them, and re-layouts: 27.9 us -> 28.1 us
where the time goes in v1:
time: 927 us; the launch traced here: 917 us
  matrix products  251 us (27%)
  local copies, waits for them, and re-layouts  204 us (22%)
  blocking collectives  126 us (14%)
  other arithmetic  122 us (13%)
  waiting for transfers between devices  109 us (12%)
  loops' own time  53.9 us (6%)
  starting transfers between devices  36.2 us (4%)
  between operations  16.7 us (2%)
    psum x1, blocking collectives, local(): lax.psum((head_parts[0], head_parts[1], grad_conv, head_parts[2], head_pa...  119 us
    all_to_all x2, waiting for transfers between devices, local(): lax.all_to_all(projected, 'mp', split_axis=2, concat_axis=0, tiled=True)  49.2 us
    all_to_all x2, waiting for transfers between devices, link_unit(): lax.all_to_all(view_out, axis_name='mp', split_axis=0, concat_axis=0)  47.2 us
    dot_general x16, matrix products, score_block(): jnp.einsum('qhd,khd->hqk', queries, key_seq, preferred_element_type=jnp.f...  39.7 us
    another operation x16, local copies, waits for them, and re-layouts, local(): jnp.stack([grad_queries.reshape(group_rows, local_width), grad_keys.resha...  39 us
    another operation x2, loops' own time, attend_backward(): lax.map(backward_block, jnp.arange(seq_count * per_seq, dtype=jnp.int32))  32.2 us
    unnamed x211, local copies, waits for them, and re-layouts  28.1 us
    dot_general x8, matrix products, backward_block(): jnp.einsum('hqk,qhd->khd', probabilities.astype(jnp.bfloat16), grad_rows,...  22.4 us
  transfers between devices with their start and end apart: 14, of which 6 were waited for; matrix products, arithmetic and copies ran while one was open for 48% of the time, Pallas kernels for 0%

profile of v1, /device:TPU:0, one launch (start us, length us, event | category | flops | bytes accessed | tf_op | source)
XLA Modules:
  0.0 917.3 jit_solution(8295530578231400474)
XLA Ops:
  15.4 6.0 copy.66
  21.4 4.7 all-to-all-start
  26.7 4.7 convolution_convert_fusion
  31.3 6.0 copy.72
  37.3 26.4 %all-to-all-done = bf16[512,3,768]{0,1,2:T(4,128)(2,1)} async-done(((bf16[512,3,768]{0,1,2:T(4,128)(2,1)}), bf16[512,3,768]{0,1,2:T(4,128)(2,1)}, u32[]{:S(2)}, u32[]{:S(2)}) %all-to-all-start) | async-done | bytes 2359328 | tf_op jit(solution)/shard_map/all_to_all | solution.py:158
  63.7 4.9 all-to-all-start.2
  82.7 22.8 %all-to-all-done.2 = bf16[512,3,768]{0,1,2:T(4,128)(2,1)} async-done(((bf16[512,3,768]{0,1,2:T(4,128)(2,1)}), bf16[512,3,768]{0,1,2:T(4,128)(2,1)}, u32[]{:S(2)}, u32[]{:S(2)}) %all-to-all-start.2) | async-done | bytes 2359328 | tf_op jit(solution)/shard_map/all_to_all | solution.py:158
  112.2 7.5 add_convert_fusion.2
  119.7 6.6 reshape.605
  134.7 49.8 %while.64 = (s32[]{:T(128)}, bf16[4,512,192]{1,2,0:T(8,128)(2,1)}, f32[4,3,512]{2,1,0:T(4,128)}, s32[4]{0:T(128)}, bf16[2,1024,3,64]{1,3,2,0:T(8,128)(2,1)}, /*i...) while((s32[]{:T(128)}, bf16[4,512,192]{1,2,0:T(8,128)(2,1)}, ...), condition=%wide.region_5.6_spmd, body=%wide.region_2.5_spmd.sunk | while | flops 423197728 | bytes 25768452 | solution.py:78
  184.5 4.2 all-to-all-start.1
  188.7 6.6 reshape.606
  203.8 49.4 %while.65 = (s32[]{:T(128)}, bf16[4,512,192]{1,2,0:T(8,128)(2,1)}, f32[4,3,512]{2,1,0:T(4,128)}, s32[4]{0:T(128)}, bf16[2,1024,3,64]{1,3,2,0:T(8,128)(2,1)}, /*i...) while((s32[]{:T(128)}, bf16[4,512,192]{1,2,0:T(8,128)(2,1)}, ...), condition=%wide.region_13.14_spmd, body=%wide.region_10.13_spmd.sunk | while | flops 423197728 | bytes 25768452 | solution.py:78
  253.2 4.2 all-to-all-start.3
  262.3 6.8 all-to-all-done.3
  272.3 4.9 fusion.234
  280.1 8.6 multiply_convert_fusion.2
  288.7 5.2 multiply_convert_fusion.3
  294.0 5.8 fusion.233
  299.8 5.6 convolution_add_fusion.1
  305.5 6.1 fusion.239
  311.7 6.7 multiply_reduce_fusion.6
  325.6 4.2 all-to-all-start.4
  335.9 5.3 fusion.168
  341.2 9.5 %convolution_add_fusion = f32[3072,768]{1,0:T(8,128)} fusion(f32[3072,768]{1,0:T(8,128)S(1)} %fusion.168, f32[512,3072]{1,0:T(8,128)} %copy-done.8, bf16[2,512,768]{2,1,0:T(8,128)(2,1)S(1)} %copy-done.28), kind=kOutput, calls=%fused_computation.141 | convolution fusion | flops 2422996992 | bytes 25952256 | tf_op jit(solution)/shard_map/rf,rd->fd/dot_general | solution.py:244
  350.7 4.6 all-to-all-start.6
  369.0 79.1 %while.66 = (s32[]{:T(128)}, f32[4,512,3,64]{1,3,2,0:T(8,128)}, f32[4,1024,3,64]{1,3,2,0:T(8,128)}, f32[4,1024,3,64]{1,3,2,0:T(8,128)}, s32[4]{0:T(128)S(1)}, /*...) while((s32[]{:T(128)}, f32[4,512,3,64]{1,3,2,0:T(8,128)}, ...), condition=%wide.region_20.21_spmd, body=%wide.region_18.20_spmd.sunk | while | flops 1032092672 | bytes 62722712 | solution.py:118
  461.7 79.5 %while.67 = (s32[]{:T(128)}, f32[4,512,3,64]{1,3,2,0:T(8,128)}, f32[4,1024,3,64]{1,3,2,0:T(8,128)}, f32[4,1024,3,64]{1,3,2,0:T(8,128)}, s32[4]{0:T(128)S(1)}, /*...) while((s32[]{:T(128)}, f32[4,512,3,64]{1,3,2,0:T(8,128)}, ...), condition=%wide.region_29.30_spmd, body=%wide.region_27.29_spmd.sunk | while | flops 1032092672 | bytes 62722712 | solution.py:118
  567.5 3.9 stack_reshape.20
  592.3 6.0 multiply_reduce_fusion.5
  598.4 6.7 multiply_reduce_fusion.3
  605.1 10.2 %fusion.111 = (bf16[2048,3,192]{0,2,1:T(8,128)(2,1)S(1)}, bf16[2048,3,192]{0,2,1:T(8,128)(2,1)}) fusion(f32[2048,3,192]{0,2,1:T(8,128)} %get-tuple-element.888, f32[2048,3,192]{0,2,1:T(8,128)} %get-tuple-element.887, f32[2048,3,192]{0,2,1:T(8,128)S(1)} %constant_dynamic-update-slice_fusion.2, f32[3,192]{1,0:T(4,128)S(1)} %copy-done.64, ...), kind=kLoop, calls=%fused_computation.154 | loop fusion | flops 14155776 | bytes 33037056 | tf_op jit(solution)/shard_map/convert_element_type | solution.py:296
  617.2 4.5 all-to-all-start.5
  625.2 25.1 %all-to-all-done.5 = bf16[4,512,3,192]{1,3,2,0:T(8,128)(2,1)} async-done(((bf16[4,512,3,192]{1,3,2,0:T(8,128)(2,1)}), bf16[4,512,3,192]{1,3,2,0:T(8,128)(2,1)}, u32[]{:S(2)}, u32[]{:S(2)}) %all-to-all-start.5) | async-done | bytes 2359328 | tf_op jit(solution)/shard_map/all_to_all | solution.py:302
  650.3 4.5 all-to-all-start.7
  663.7 22.2 %all-to-all-done.7 = bf16[4,512,3,192]{1,3,2,0:T(8,128)(2,1)} async-done(((bf16[4,512,3,192]{1,3,2,0:T(8,128)(2,1)}), bf16[4,512,3,192]{1,3,2,0:T(8,128)(2,1)}, u32[]{:S(2)}, u32[]{:S(2)}) %all-to-all-start.7) | async-done | bytes 2359328 | tf_op jit(solution)/shard_map/all_to_all | solution.py:302
  690.5 4.4 add_convert_fusion
  699.6 8.1 fusion.167
  707.8 6.8 fusion.166
  716.9 3.8 stack.114
  739.4 3.9 fusion.238
  743.4 5.1 fusion.154
  749.7 6.9 all-reduce.17
  764.4 4.0 fusion.144
  770.4 118.9 %all-reduce.19 = (f32[192]{0:T(256)}, f32[192]{0:T(256)}, f32[768,3,192]{0,2,1:T(8,128)}, f32[3,3,192]{2,0,1:T(4,128)}, f32[192,768]{1,0:T(8,128)}, /*index=5*/f32[192]{0:T(256)}, f32[192]{0:T(256)}) all-reduce(f32[192]{0:T(256)S(1)} %copy-done.92, f32[192]{0:T(256)} %dynamic-slice_convert_fusion.2, ...), channel_id=1, replica_groups=mesh['dp'=8,'mp'=4] {'dp'}, use_global_device_ids=true, to_apply=%region_37.38 | all-reduce | flops 592320 | bytes 3558912 | tf_op jit(solution)/shard_map/psum | solution.py:338
  890.6 7.5 copy.109
  898.1 5.1 all-gather.5.cloned.1.call-done
  903.2 6.8 convert_element_type.321
  (589 shorter events, 404.6 us)
Async XLA Ops:
  9.0 17.0 %copy-start.71 = (f32[512]{0:T(512)}, f32[512]{0:T(512)S(1)}, u32[]{:S(2)}) copy-start(f32[512]{0:T(512)S(1)} %get-tuple-element.940) | copy-start | bytes 6148
  21.4 42.3 %all-to-all-start = ((bf16[512,3,768]{0,1,2:T(4,128)(2,1)}), bf16[512,3,768]{0,1,2:T(4,128)(2,1)}, u32[]{:S(2)}, u32[]{:S(2)}) async-start(bf16[512,3,768]{0,1,2:T(4,128)(2,1)} %copy.66), calls=%async_computation | async-start | bytes 6291456 | tf_op jit(solution)/shard_map/all_to_all | solution.py:158
  37.3 31.2 %copy-start.88 = (f32[3,3,192]{2,1,0:T(4,128)S(1)}, f32[3,3,192]{2,1,0:T(4,128)}, u32[]{:S(2)}) copy-start(f32[3,3,192]{2,1,0:T(4,128)} %param.25) | copy-start | bytes 20740
  63.7 41.8 %all-to-all-start.2 = ((bf16[512,3,768]{0,1,2:T(4,128)(2,1)}), bf16[512,3,768]{0,1,2:T(4,128)(2,1)}, u32[]{:S(2)}, u32[]{:S(2)}) async-start(bf16[512,3,768]{0,1,2:T(4,128)(2,1)} %copy.72), calls=%async_computation.2 | async-start | bytes 6291456 | tf_op jit(solution)/shard_map/all_to_all | solution.py:158
  110.7 9.0 copy-start.3
  184.5 68.7 %all-to-all-start.1 = ((bf16[4,512,192]{1,2,0:T(8,128)(2,1)}), bf16[4,512,192]{1,2,0:T(8,128)(2,1)}, u32[]{:S(2)}, u32[]{:S(2)}) async-start(bf16[4,512,192]{1,2,0:T(8,128)(2,1)} %get-tuple-element.653), calls=%async_computation.1 | async-start | bytes 1572864 | tf_op jit(solution)/shard_map/all_to_all | solution.py:181
  253.2 7.1 copy-start.46
  253.2 15.9 %all-to-all-start.3 = ((bf16[4,512,192]{1,2,0:T(8,128)(2,1)}), bf16[4,512,192]{1,2,0:T(8,128)(2,1)}, u32[]{:S(2)}, u32[]{:S(2)}) async-start(bf16[4,512,192]{1,2,0:T(8,128)(2,1)} %get-tuple-element.654), calls=%async_computation.3 | async-start | bytes 1572864 | tf_op jit(solution)/shard_map/all_to_all | solution.py:181
  257.4 437.5 %reduce-scatter.9.cloned.1.call-start = ((), (), s32[]{:S(2)}) async-start(), calls=%async_computation.14 | async-start | bytes 9732096 | tf_op jit(solution)/shard_map/reduce_scatter | solution.py:351
  269.1 8.1 slice-start.6
  271.9 22.0 %copy-start.29 = (f32[512,768]{1,0:T(8,128)}, f32[512,768]{1,0:T(8,128)S(1)}, u32[]{:S(2)}) copy-start(f32[512,768]{1,0:T(8,128)S(1)} %get-tuple-element.935) | copy-start | bytes 4718596
  271.9 22.0 %copy-start.69 = (f32[512]{0:T(512)}, f32[512]{0:T(512)S(1)}, u32[]{:S(2)}) copy-start(f32[512]{0:T(512)S(1)} %broadcast_multiply_fusion.12) | copy-start | bytes 6148
  272.3 21.7 %copy-start.86 = (f32[512]{0:T(512)}, f32[512]{0:T(512)S(1)}, u32[]{:S(2)}) copy-start(f32[512]{0:T(512)S(1)} %add_rsqrt_fusion) | copy-start | bytes 6148
  280.1 8.6 copy-start.8
  294.0 5.8 copy-start.40
  305.4 6.2 copy-start.18
  305.5 6.2 copy-start.30
  305.5 6.2 copy-start.41
  305.5 6.1 copy-start.60
  305.5 6.1 copy-start.68
  305.5 6.1 copy-start.70
  305.5 6.1 copy-start.87
  311.7 6.7 copy-start.27
  325.6 25.0 %all-to-all-start.4 = ((bf16[512,4,192]{0,2,1:T(8,128)(2,1)}), bf16[512,4,192]{0,2,1:T(8,128)(2,1)}, u32[]{:S(2)}, u32[]{:S(2)}) async-start(bf16[512,4,192]{0,2,1:T(8,128)(2,1)} %bitcast.529), calls=%async_computation.4 | async-start | bytes 1572864 | tf_op jit(solution)/shard_map/all_to_all | solution.py:270
  329.9 366.8 %reduce-scatter.11.cloned.1.call-start = ((), (), s32[]{:S(2)}) async-start(), calls=%async_computation.16 | async-start | bytes 9732096 | tf_op jit(solution)/shard_map/reduce_scatter | solution.py:352
  335.9 5.3 copy-start.28
  350.7 97.3 %all-to-all-start.6 = ((bf16[512,4,192]{0,2,1:T(8,128)(2,1)}), bf16[512,4,192]{0,2,1:T(8,128)(2,1)}, u32[]{:S(2)}, u32[]{:S(2)}) async-start(bf16[512,4,192]{0,2,1:T(8,128)(2,1)} %bitcast.528), calls=%async_computation.6 | async-start | bytes 1572864 | tf_op jit(solution)/shard_map/all_to_all | solution.py:270
  541.2 5.0 copy-start.20
  586.3 5.8 slice-start.4
  591.6 6.8 slice-start.2
  592.3 6.0 slice-start.3
  592.3 6.0 copy-start.50
  592.3 6.0 copy-start.52
  598.4 6.8 copy-start.62
  598.4 6.8 copy-start.64
  598.4 6.7 copy-start.66
  617.2 33.1 %all-to-all-start.5 = ((bf16[4,512,3,192]{1,3,2,0:T(8,128)(2,1)}), bf16[4,512,3,192]{1,3,2,0:T(8,128)(2,1)}, u32[]{:S(2)}, u32[]{:S(2)}) async-start(bf16[4,512,3,192]{1,3,2,0:T(8,128)(2,1)} %pad_maximum_fusion.1), calls=%async_computation.5 | async-start | bytes 4718592 | tf_op jit(solution)/shard_map/all_to_all | solution.py:302
  650.3 35.6 %all-to-all-start.7 = ((bf16[4,512,3,192]{1,3,2,0:T(8,128)(2,1)}), bf16[4,512,3,192]{1,3,2,0:T(8,128)(2,1)}, u32[]{:S(2)}, u32[]{:S(2)}) async-start(bf16[4,512,3,192]{1,3,2,0:T(8,128)(2,1)} %pad_maximum_fusion.2), calls=%async_computation.7 | async-start | bytes 4718592 | tf_op jit(solution)/shard_map/all_to_all | solution.py:302
  654.8 84.6 %reduce-scatter.7.cloned.1.call-start = ((), (), s32[]{:S(2)}) async-start(), calls=%async_computation.13 | async-start | bytes 1474560 | tf_op jit(solution)/shard_map/reduce_scatter | solution.py:322
  660.4 110.0 %reduce-scatter.5.cloned.1.call-start = ((), (), s32[]{:S(2)}) async-start(), calls=%async_computation.12 | async-start | bytes 4423680 | tf_op jit(solution)/shard_map/reduce_scatter | solution.py:319
  663.7 24.2 %copy-start.72 = (f32[512]{0:T(512)S(1)}, f32[512]{0:T(512)}, u32[]{:S(2)}) copy-start(f32[512]{0:T(512)} %copy-done.71) | copy-start | bytes 6148
  663.7 24.3 %copy-start.84 = (f32[512]{0:T(512)S(1)}, f32[512]{0:T(512)}, u32[]{:S(2)}) copy-start(f32[512]{0:T(512)} %copy-done.83) | copy-start | bytes 6148
  663.7 24.3 %copy-start.90 = (f32[768]{0:T(1024)S(1)}, f32[768]{0:T(1024)}, u32[]{:S(2)}) copy-start(f32[768]{0:T(1024)} %param.22) | copy-start | bytes 9220
  663.7 24.3 %copy-start.99 = (f32[768]{0:T(1024)S(1)}, f32[768]{0:T(1024)}, u32[]{:S(2)}) copy-start(f32[768]{0:T(1024)} %param.23) | copy-start | bytes 9220
  694.9 195.7 %all-gather.3.cloned.1.call-start = ((), (), s32[]{:S(2)}) async-start(), calls=%async_computation.15 | async-start | bytes 4866048 | tf_op jit(solution)/shard_map/all_gather | solution.py:355
  696.6 206.6 %all-gather.5.cloned.1.call-start = ((), (), s32[]{:S(2)}) async-start(), calls=%async_computation.17 | async-start | bytes 4866048 | tf_op jit(solution)/shard_map/all_gather | solution.py:358
  699.6 8.1 copy-start.19
  743.4 5.1 copy-start.45
  (99 other events, 235.1 us)
Sparse Core Ops, SparseCore 0:
  305.6 141.3 reduce-scatter.8
  453.5 135.0 reduce-scatter.10
  660.6 30.0 reduce-scatter.6
  695.0 42.4 reduce-scatter.4
  740.3 82.9 all-gather.2
  826.0 77.1 all-gather.4
